TPU v7x, 32 devices: a whole 2x2x4 slice. The times are simulated.
32 devices in a mesh: seg: 8 (over z, core), bond: 4 (over y, x).
Axes of the slice: x: 2, y: 2, z: 4, core: 2. Of those that a mesh axis runs over, the one named last changes fastest.
Arguments:
- left_env: bfloat16 [8, 1024, 6, 1024], P('seg', 'bond'), may hold values from -0.1875 to 0.1875
- prev_left: bfloat16 [8, 1024, 1024], P('seg'), may hold values from -0.25 to 1.25
- cur_site: bfloat16 [8, 1024, 4, 1024], P('seg', 'bond'), may hold values from -6 to 6
- prev_site: bfloat16 [8, 1024, 4, 1024], P('seg', None, None, 'bond'), may hold values from -6 to 6
- hamiltonian: bfloat16 [8, 6, 6, 4, 4], P('seg'), may hold values from -1.25 to 1.25
- right_env: bfloat16 [8, 1024, 6, 1024], P('seg', 'bond'), may hold values from -0.078125 to 0.078125
- prev_right: bfloat16 [8, 1024, 1024], P('seg'), may hold values from -0.25 to 1.25
Outputs:
- new_site: bfloat16 [8, 1024, 4, 1024], P('seg', 'bond')
- center: float32 [8, 1024, 1024], P('seg', 'bond')
All inputs are finite; a program needn't handle non-finite values.
Results may differ from a plain program's by a relative error of at most 0.0054.
Values may be sent and summed in bfloat16 or wider, within the bound.
A program may use at most 128 MiB of HBM per device.

v0:
```python
import math
import jax
import jax.numpy as jnp
from jax import lax
from jax.sharding import PartitionSpec as P

PHYS = 4
MPOB = 6


def shifted(block, axis, distance):
    devices = range(lax.axis_size(axis))
    route = [((i - distance) % len(devices), i) for i in devices]
    return lax.ppermute(block, axis, route)


def shards(left_env, prev_left, cur_site, prev_site, hamiltonian, right_env, prev_right):
    left_now, prev_now = shifted((left_env[0], prev_left[0]), "seg", 1)
    own_rows = left_now.shape[0]
    bond_width = left_now.shape[2]
    coupling = hamiltonian[0].astype(jnp.float32)
    current = lax.all_gather(cur_site[0], "bond", axis=0, tiled=True)
    projected = jnp.dot(
        left_now.reshape(own_rows * MPOB, bond_width),
        current.reshape(bond_width, PHYS * bond_width),
        preferred_element_type=jnp.float32,
    ).reshape(own_rows, MPOB, PHYS, bond_width)
    mixture = jnp.einsum(
        "autc,uvst->asvc", projected, coupling, precision=lax.Precision.HIGHEST
    ).astype(jnp.bfloat16)
    applied = jnp.einsum(
        "asvc,cvy->asy",
        mixture,
        lax.all_gather(right_env[0], "bond", axis=0, tiled=True),
        preferred_element_type=jnp.float32,
    )
    partial_value = jnp.einsum(
        "ab,bsc->asc", prev_now, prev_site[0], preferred_element_type=jnp.float32
    ).astype(jnp.bfloat16)
    second = jnp.einsum(
        "akc,cy->aky",
        lax.all_to_all(partial_value, "bond", split_axis=0, concat_axis=2, tiled=True),
        prev_right[0],
        preferred_element_type=jnp.float32,
    )
    target = (2.0 * applied - second).reshape(own_rows * PHYS, bond_width)
    local_correlation = jnp.dot(
        target.T, target, precision=lax.Precision.HIGHEST, preferred_element_type=jnp.float32
    )
    correlation = lax.psum(local_correlation, "bond")
    triangle = jnp.linalg.cholesky(correlation)
    solved = jax.scipy.linalg.solve_triangular(triangle, target.T, lower=True)
    norming = math.sqrt(bond_width * PHYS)
    new_site = (solved.T * norming).astype(jnp.bfloat16).reshape(1, own_rows, PHYS, bond_width)
    offset = lax.axis_index("bond") * own_rows
    center = lax.dynamic_slice_in_dim(triangle.T, offset, own_rows, 0) / norming
    return (new_site, center[None])


def solution(mesh):
    return jax.shard_map(
        shards,
        mesh=mesh,
        in_specs=(
            P("seg", "bond", None, None),
            P("seg", None, None),
            P("seg", "bond", None, None),
            P("seg", None, None, "bond"),
            P("seg", None, None, None, None),
            P("seg", "bond", None, None),
            P("seg", None, None),
        ),
        out_specs=(P("seg", "bond", None, None), P("seg", "bond", None)),
        check_vma=False,
    )
```

profile of v0, /device:TPU:0, one launch (start us, length us, event | category | flops | bytes accessed | tf_op | source)
XLA Modules:
  0.0 759.1 jit_solution(3926485406650583413)
XLA Ops:
  11.9 25.3 %collective-permute-done.1 = bf16[1024,1024]{1,0:T(8,128)(2,1)S(1)} collective-permute-done((bf16[1024,1024]{1,0:T(8,128)(2,1)}, bf16[1024,1024]{1,0:T(8,128)(2,1)S(1)}, u32[]{:S(2)}, u32[]{:S(2)}) %collective-permute-start.1) | collective-permute-done | bytes 2097184 | tf_op jit(solution)/shard_map/ppermute | solution.py:14
  41.2 40.1 %all_to_all.18 = bf16[1024,4,256]{2,1,0:T(4,128)(2,1)S(1)} all-to-all(bf16[1024,4,256]{2,1,0:T(4,128)(2,1)S(1)} %copy.30), channel_id=1, replica_groups=mesh['seg'=8,'bond'=4] {'bond'}, dimensions={0} | all-to-all | bytes 4194304 | tf_op jit(solution)/shard_map/all_to_all | solution.py:42
  85.6 6.5 fusion.26
  92.1 22.9 %all-gather.5.cloned.1.call-done = bf16[1,1024,4,1024]{3,2,0,1:T(4,128)(2,1)} async-done(((bf16[1,256,4,1024]{3,2,0,1:T(4,128)(2,1)}), bf16[1,1024,4,1024]{3,2,0,1:T(4,128)(2,1)}) %all-gather.5.cloned.1.call-update) | async-done | bytes 8388624 | tf_op jit(solution)/shard_map/all_gather | solution.py:22
  115.0 14.1 %copy.45 = bf16[1,1024,4,1024]{1,3,2,0:T(8,128)(2,1)} copy(bf16[1,1024,4,1024]{3,2,0,1:T(4,128)(2,1)} %all-gather.5.cloned.1.call-done) | data formatting | bytes 16777216 | tf_op jit(solution)/shard_map/reshape | solution.py:25
  129.1 21.9 %convolution_bitcast_fusion = f32[256,6,4,1024,1]{3,0,2,1,4:T(8,128)} fusion(bf16[1,1024,4,1024]{1,3,2,0:T(8,128)(2,1)} %copy.45, bf16[256,6,1024]{2,0,1:T(8,128)(2,1)} %collective-permute-done), kind=kOutput, calls=%fused_computation.9 | convolution fusion | flops 12884901888 | bytes 36700160 | tf_op jit(solution)/shard_map/dot_general | solution.py:23
  151.0 62.8 %fusion.2 = bf16[256,4,6,1024]{3,2,1,0:T(8,128)(2,1)} fusion(f32[256,6,4,1024,1]{3,0,2,1,4:T(8,128)} %convolution_bitcast_fusion, bf16[1,6,6,4,4]{2,4,3,1,0:T(4,128)(2,1)S(1)} %copy-done.5), kind=kOutput, calls=%fused_computation.5 | convolution fusion | flops 1818230784 | bytes 37749888 | tf_op jit(solution)/shard_map/autc,uvst->asvc/dot_general | solution.py:28
  213.7 25.5 %all-gather.7.cloned.1.call-done = bf16[1,1024,6,1024]{3,1,2,0:T(8,128)(2,1)} async-done(((bf16[1,256,6,1024]{3,1,2,0:T(8,128)(2,1)}), bf16[1,1024,6,1024]{3,1,2,0:T(8,128)(2,1)}) %all-gather.7.cloned.1.call-update) | async-done | bytes 12582928 | tf_op jit(solution)/shard_map/all_gather | solution.py:34
  239.2 32.4 %fusion.10 = f32[256,4,1024]{2,0,1:T(8,128)S(1)} fusion(f32[256,4,1024]{2,0,1:T(8,128)} %fusion.26, bf16[1,1024,6,1024]{3,1,2,0:T(8,128)(2,1)} %all-gather.7.cloned.1.call-done, bf16[256,4,6,1024]{3,2,1,0:T(8,128)(2,1)} %fusion.2), kind=kOutput, calls=%fused_computation.14 | convolution fusion | flops 12886999040 | bytes 33554432 | tf_op jit(solution)/shard_map/asvc,cvy->asy/dot_general | solution.py:31
  273.6 15.1 %convolution_bitcast_fusion.1 = f32[1024,1024]{0,1:T(8,128)} fusion(f32[256,4,1024]{2,0,1:T(8,128)S(1)} %fusion.10), kind=kOutput, calls=%fused_computation.20 | convolution fusion | flops 12884901888 | bytes 8388608 | tf_op jit(solution)/shard_map/dot_general | solution.py:47
  288.8 6.8 copy.35
  300.9 5.5 copy.36
  306.4 86.1 %all-reduce.3.cloned.1.call-done = f32[1024,1024]{0,1:T(8,128)} async-done(((f32[1024,1024]{0,1:T(8,128)}), f32[1024,1024]{0,1:T(8,128)}) %all-reduce.3.cloned.1.call-update) | async-done | bytes 4194320 | tf_op jit(solution)/shard_map/psum | solution.py:50
  392.5 5.7 copy.34
  404.7 11.7 %cholesky.223 = f32[128,128]{1,0:T(8,128)S(1)} custom-call(f32[128,128]{1,0:T(8,128)S(1)} %cholesky.580), custom_call_target="Cholesky" | custom-call | tf_op jit(solution)/shard_map/jit(cholesky)/cholesky | solution.py:51
  416.4 9.8 %custom-call.63 = f32[1,128,128]{1,2,0:T(8,128)S(1)} custom-call(f32[1,128,128]{2,1,0:T(8,128)S(1)} %get-tuple-element.74), custom_call_target="InvertDiagBlocksLowerTriangular" | custom-call | tf_op jit(solution)/shard_map/jit(cholesky)/cholesky | solution.py:51
  432.7 11.9 %cholesky.244 = f32[128,128]{1,0:T(8,128)S(1)} custom-call(f32[128,128]{1,0:T(8,128)S(1)} %cholesky.584), custom_call_target="Cholesky" | custom-call | tf_op jit(solution)/shard_map/jit(cholesky)/cholesky | solution.py:51
  445.2 9.8 %custom-call.64 = f32[1,128,128]{1,2,0:T(8,128)S(1)} custom-call(f32[1,128,128]{2,1,0:T(8,128)S(1)} %get-tuple-element.71), custom_call_target="InvertDiagBlocksLowerTriangular" | custom-call | tf_op jit(solution)/shard_map/jit(cholesky)/cholesky | solution.py:51
  458.4 11.7 %cholesky.468 = f32[128,128]{1,0:T(8,128)S(1)} custom-call(f32[128,128]{1,0:T(8,128)S(1)} %cholesky.589), custom_call_target="Cholesky" | custom-call | tf_op jit(solution)/shard_map/jit(cholesky)/cholesky | solution.py:51
  471.4 9.8 %custom-call.65 = f32[1,128,128]{1,2,0:T(8,128)S(1)} custom-call(f32[1,128,128]{2,1,0:T(8,128)S(1)} %get-tuple-element.68), custom_call_target="InvertDiagBlocksLowerTriangular" | custom-call | tf_op jit(solution)/shard_map/jit(cholesky)/cholesky | solution.py:51
  484.7 11.9 %cholesky.487 = f32[128,128]{1,0:T(8,128)S(1)} custom-call(f32[128,128]{1,0:T(8,128)S(1)} %cholesky.594), custom_call_target="Cholesky" | custom-call | tf_op jit(solution)/shard_map/jit(cholesky)/cholesky | solution.py:51
  497.9 9.8 %custom-call.66 = f32[1,128,128]{1,2,0:T(8,128)S(1)} custom-call(f32[1,128,128]{2,1,0:T(8,128)S(1)} %get-tuple-element.65), custom_call_target="InvertDiagBlocksLowerTriangular" | custom-call | tf_op jit(solution)/shard_map/jit(cholesky)/cholesky | solution.py:51
  511.2 11.7 %cholesky.506 = f32[128,128]{1,0:T(8,128)S(1)} custom-call(f32[128,128]{1,0:T(8,128)S(1)} %cholesky.599), custom_call_target="Cholesky" | custom-call | tf_op jit(solution)/shard_map/jit(cholesky)/cholesky | solution.py:51
  524.2 10.2 %custom-call.67 = f32[1,128,128]{1,2,0:T(8,128)S(1)} custom-call(f32[1,128,128]{2,1,0:T(8,128)S(1)} %get-tuple-element.62), custom_call_target="InvertDiagBlocksLowerTriangular" | custom-call | tf_op jit(solution)/shard_map/jit(cholesky)/cholesky | solution.py:51
  537.7 11.7 %cholesky.526 = f32[128,128]{1,0:T(8,128)S(1)} custom-call(f32[128,128]{1,0:T(8,128)S(1)} %cholesky.604), custom_call_target="Cholesky" | custom-call | tf_op jit(solution)/shard_map/jit(cholesky)/cholesky | solution.py:51
  550.7 9.8 %custom-call.68 = f32[1,128,128]{1,2,0:T(8,128)S(1)} custom-call(f32[1,128,128]{2,1,0:T(8,128)S(1)} %get-tuple-element.59), custom_call_target="InvertDiagBlocksLowerTriangular" | custom-call | tf_op jit(solution)/shard_map/jit(cholesky)/cholesky | solution.py:51
  563.5 11.9 %cholesky.546 = f32[128,128]{1,0:T(8,128)S(1)} custom-call(f32[128,128]{1,0:T(8,128)S(1)} %cholesky.609), custom_call_target="Cholesky" | custom-call | tf_op jit(solution)/shard_map/jit(cholesky)/cholesky | solution.py:51
  576.6 9.8 %custom-call.69 = f32[1,128,128]{1,2,0:T(8,128)S(1)} custom-call(f32[1,128,128]{2,1,0:T(8,128)S(1)} %get-tuple-element.56), custom_call_target="InvertDiagBlocksLowerTriangular" | custom-call | tf_op jit(solution)/shard_map/jit(cholesky)/cholesky | solution.py:51
  589.0 11.7 %cholesky.564 = f32[128,128]{1,0:T(8,128)S(1)} custom-call(f32[128,128]{1,0:T(8,128)S(1)} %convolution_subtract_fusion.11), custom_call_target="Cholesky" | custom-call | tf_op jit(solution)/shard_map/jit(cholesky)/cholesky | solution.py:51
  607.6 6.7 fusion.11
  614.3 23.0 %while.1 = (s32[]{:T(128)}, f32[1024,1024]{1,0:T(8,128)}, s32[8,2]{0,1:T(2,128)S(1)}, f32[8,128,128]{2,1,0:T(8,128)S(1)}, s32[]{:T(128)}) while((s32[]{:T(128)}, f32[1024,1024]{1,0:T(8,128)}, s32[8,2]{0,1:T(2,128)S(1)}, f32[8,128,128]{2,1,0:T(8,128)S(1)}, s32[]{:T(128)}) %tuple.65), condition=%wide.while_cond, body=%wide.while_body.sunk | while | flops 2 | bytes 131181 | solution.py:52
  637.3 78.8 %custom-call.70 = f32[8,128,128]{1,2,0:T(8,128)S(1)} custom-call(f32[8,128,128]{2,1,0:T(8,128)S(1)} %get-tuple-element.9), custom_call_target="InvertDiagBlocksLowerTriangular" | custom-call | tf_op jit(solution)/shard_map/jit(_solve_triangular)/triangular_solve | solution.py:52
  (111 shorter events, 120.3 us)
Async XLA Ops:
  7.2 30.0 %copy-start = (bf16[1,1024,4,256]{3,2,1,0:T(4,128)(2,1)S(1)}, bf16[1,1024,4,256]{3,2,1,0:T(4,128)(2,1)}, u32[]{:S(2)}) copy-start(bf16[1,1024,4,256]{3,2,1,0:T(4,128)(2,1)} %param.10) | copy-start | bytes 6291460
  7.2 107.8 %all-gather.5.cloned.1.call-start = ((), (), s32[]{:S(2)}) async-start(), calls=%async_computation.2 | async-start | bytes 10485760 | tf_op jit(solution)/shard_map/all_gather | solution.py:22
  7.9 231.3 %all-gather.7.cloned.1.call-start = ((), (), s32[]{:S(2)}) async-start(), calls=%async_computation.3 | async-start | bytes 15728640 | tf_op jit(solution)/shard_map/all_gather | solution.py:34
  8.7 383.9 %all-reduce.3.cloned.1.call-start = ((), (), s32[]{:S(2)}) async-start(), calls=%async_computation.1 | async-start | bytes 8388608 | tf_op jit(solution)/shard_map/psum | solution.py:50
  8.7 28.5 %collective-permute-start.1 = (bf16[1024,1024]{1,0:T(8,128)(2,1)}, bf16[1024,1024]{1,0:T(8,128)(2,1)S(1)}, u32[]{:S(2)}, u32[]{:S(2)}) collective-permute-start(bf16[1024,1024]{1,0:T(8,128)(2,1)} %bitcast.186), channel_id=1, source_target_pairs={{28,0},{0,4},{4,8},{8,12},{12,16},{16,20},{20,24},{24,28},{29,1},{... | collective-permute-start | bytes 6291464 | tf_op jit(solution)/shard_map/ppermute | solution.py:14
  9.3 119.9 %collective-permute-start = (bf16[256,6,1024]{2,0,1:T(8,128)(2,1)}, bf16[256,6,1024]{2,0,1:T(8,128)(2,1)}, u32[]{:S(2)}, u32[]{:S(2)}) collective-permute-start(bf16[256,6,1024]{2,0,1:T(8,128)(2,1)} %bitcast.185), channel_id=1, source_target_pairs={{28,0},{0,4},{4,8},{8,12},{12,16},{16,20},{20,24},{24,28},{29,1},{... | collective-permute-start | bytes 9437192 | tf_op jit(solution)/shard_map/ppermute | solution.py:14
  129.1 21.9 %copy-start.5 = (bf16[1,6,6,4,4]{2,4,3,1,0:T(4,128)(2,1)S(1)}, bf16[1,6,6,4,4]{2,4,3,1,0:T(4,128)(2,1)}, u32[]{:S(2)}) copy-start(bf16[1,6,6,4,4]{2,4,3,1,0:T(4,128)(2,1)} %param.11) | copy-start | bytes 3460
  271.7 1.9 copy-start.4
  402.7 2.0 copy-start.3
  716.2 4.3 copy-start.2
  741.5 10.8 %copy-start.1 = (bf16[1,1024,4,256]{3,2,1,0:T(4,128)(2,1)S(1)}, bf16[1,1024,4,256]{3,2,1,0:T(4,128)(2,1)}, u32[]{:S(2)}) copy-start(bf16[1,1024,4,256]{3,2,1,0:T(4,128)(2,1)} %param.10) | copy-start | bytes 6291460
Sparse Core Ops, SparseCore 0:
  9.8 105.0 all-gather.4
  116.8 122.3 all-gather.6
  288.9 103.5 all-reduce.2
where the time goes:
time: 764 us; the launch traced here: 759 us
  other arithmetic  265 us (35%)
  matrix products  187 us (24%)
  waiting for transfers between devices  161 us (21%)
  local copies, waits for them, and re-layouts  82.3 us (11%)
  blocking collectives  40.1 us (5%)
  between operations  19.3 us (3%)
    another operation x30, other arithmetic, shards(): triangle = jnp.linalg.cholesky(correlation)  172 us
    psum x1, waiting for transfers between devices, shards(): correlation = lax.psum(local_correlation, 'bond')  86.1 us
    another operation x3, other arithmetic, shards(): solved = jax.scipy.linalg.solve_triangular(triangle, target.T, lower=True)  85.5 us
    dot_general x1, matrix products, shards(): jnp.einsum('autc,uvst->asvc', projected, coupling, precision=lax.Precisio...  62.8 us
    all_to_all x1, blocking collectives, shards(): lax.all_to_all(partial_value, 'bond', split_axis=0, concat_axis=2, tiled=...  40.1 us
    dot_general x1, matrix products, shards(): jnp.einsum('asvc,cvy->asy', mixture, lax.all_gather(right_env[0], 'bond',...  32.4 us
    all_gather x1, waiting for transfers between devices, shards(): lax.all_gather(right_env[0], 'bond', axis=0, tiled=True)  25.5 us
    ppermute x2, waiting for transfers between devices, shifted(): return lax.ppermute(block, axis, route)  25.3 us
  transfers between devices with their start and end apart: 5, of which 4 were waited for; matrix products, arithmetic and copies ran while one was open for 17% of the time, Pallas kernels for 0%

commit v1 on v0

--- a/solution.py
+++ b/solution.py
@@ -47,7 +47,11 @@
     local_correlation = jnp.dot(
         target.T, target, precision=lax.Precision.HIGHEST, preferred_element_type=jnp.float32
     )
-    correlation = lax.psum(local_correlation, "bond")
+    correlation = local_correlation
+    for hop in (1, 2):
+        correlation = correlation + lax.ppermute(
+            correlation, "bond", [(dev, dev ^ hop) for dev in range(4)]
+        )
     triangle = jnp.linalg.cholesky(correlation)
     solved = jax.scipy.linalg.solve_triangular(triangle, target.T, lower=True)
     norming = math.sqrt(bond_width * PHYS)

time: 764 us -> 852 us (1.12)
  waiting for transfers between devices: 161 us -> 238 us
  other arithmetic: 265 us -> 275 us
    ppermute x0 -> x2, waiting for transfers between devices: none -> 163 us  [shards(): lax.ppermute(correlation, 'bond', [(dev, dev ^ hop) for dev in range(4)])]
    psum x1 -> x0, waiting for transfers between devices: 86.1 us -> none  [shards(): correlation = lax.psum(local_correlation, 'bond')]
    add x0 -> x2, other arithmetic: none -> 9.71 us  [shards(): correlation + lax.ppermute(correlation, 'bond', [(dev, dev ^ hop) for dev...]
  transfers between devices with their start and end apart: 5 -> 6, of which waited for: 4 -> 5; matrix products, arithmetic and copies ran while one was open for 17% -> 15% of each run, Pallas kernels for 0% -> 0%
where the time goes in v1:
time: 852 us; the launch traced here: 847 us
  other arithmetic  275 us (32%)
  waiting for transfers between devices  238 us (28%)
  matrix products  187 us (22%)
  local copies, waits for them, and re-layouts  80 us (9%)
  blocking collectives  40.4 us (5%)
  between operations  19.5 us (2%)
    another operation x30, other arithmetic, shards(): triangle = jnp.linalg.cholesky(correlation)  172 us
    ppermute x2, waiting for transfers between devices, shards(): lax.ppermute(correlation, 'bond', [(dev, dev ^ hop) for dev in range(4)])  163 us
    another operation x3, other arithmetic, shards(): solved = jax.scipy.linalg.solve_triangular(triangle, target.T, lower=True)  85.7 us
    dot_general x1, matrix products, shards(): jnp.einsum('autc,uvst->asvc', projected, coupling, precision=lax.Precisio...  62.9 us
    all_to_all x1, blocking collectives, shards(): lax.all_to_all(partial_value, 'bond', split_axis=0, concat_axis=2, tiled=...  40.4 us
    dot_general x1, matrix products, shards(): jnp.einsum('asvc,cvy->asy', mixture, lax.all_gather(right_env[0], 'bond',...  32.4 us
    all_gather x1, waiting for transfers between devices, shards(): lax.all_gather(right_env[0], 'bond', axis=0, tiled=True)  25.3 us
    ppermute x2, waiting for transfers between devices, shifted(): return lax.ppermute(block, axis, route)  25.3 us
  transfers between devices with their start and end apart: 6, of which 5 were waited for; matrix products, arithmetic and copies ran while one was open for 15% of the time, Pallas kernels for 0%

profile of v1, /device:TPU:0, one launch (start us, length us, event | category | flops | bytes accessed | tf_op | source)
XLA Modules:
  0.0 846.8 jit_solution(2606033033993808745)
XLA Ops:
  11.9 25.3 %collective-permute-done.1 = bf16[1024,1024]{1,0:T(8,128)(2,1)S(1)} collective-permute-done((bf16[1024,1024]{1,0:T(8,128)(2,1)}, bf16[1024,1024]{1,0:T(8,128)(2,1)S(1)}, u32[]{:S(2)}, u32[]{:S(2)}) %collective-permute-start.1) | collective-permute-done | bytes 2097184 | tf_op jit(solution)/shard_map/ppermute | solution.py:14
  41.1 40.4 %all_to_all.18 = bf16[1024,4,256]{2,1,0:T(4,128)(2,1)S(1)} all-to-all(bf16[1024,4,256]{2,1,0:T(4,128)(2,1)S(1)} %copy.32), channel_id=1, replica_groups=mesh['seg'=8,'bond'=4] {'bond'}, dimensions={0} | all-to-all | bytes 4194304 | tf_op jit(solution)/shard_map/all_to_all | solution.py:42
  85.8 6.5 fusion.26
  92.3 22.6 %all-gather.5.cloned.1.call-done = bf16[1,1024,4,1024]{3,2,0,1:T(4,128)(2,1)} async-done(((bf16[1,256,4,1024]{3,2,0,1:T(4,128)(2,1)}), bf16[1,1024,4,1024]{3,2,0,1:T(4,128)(2,1)}) %all-gather.5.cloned.1.call-update) | async-done | bytes 8388624 | tf_op jit(solution)/shard_map/all_gather | solution.py:22
  115.0 14.1 %copy.48 = bf16[1,1024,4,1024]{1,3,2,0:T(8,128)(2,1)} copy(bf16[1,1024,4,1024]{3,2,0,1:T(4,128)(2,1)} %all-gather.5.cloned.1.call-done) | data formatting | bytes 16777216 | tf_op jit(solution)/shard_map/reshape | solution.py:25
  129.1 21.9 %convolution_bitcast_fusion = f32[256,6,4,1024,1]{3,0,2,1,4:T(8,128)} fusion(bf16[1,1024,4,1024]{1,3,2,0:T(8,128)(2,1)} %copy.48, bf16[256,6,1024]{2,0,1:T(8,128)(2,1)} %collective-permute-done), kind=kOutput, calls=%fused_computation.9 | convolution fusion | flops 12884901888 | bytes 36700160 | tf_op jit(solution)/shard_map/dot_general | solution.py:23
  151.0 62.9 %fusion.2 = bf16[256,4,6,1024]{3,2,1,0:T(8,128)(2,1)} fusion(f32[256,6,4,1024,1]{3,0,2,1,4:T(8,128)} %convolution_bitcast_fusion, bf16[1,6,6,4,4]{2,4,3,1,0:T(4,128)(2,1)S(1)} %copy-done.5), kind=kOutput, calls=%fused_computation.5 | convolution fusion | flops 1818230784 | bytes 37749888 | tf_op jit(solution)/shard_map/autc,uvst->asvc/dot_general | solution.py:28
  213.9 25.3 %all-gather.7.cloned.1.call-done = bf16[1,1024,6,1024]{3,1,2,0:T(8,128)(2,1)} async-done(((bf16[1,256,6,1024]{3,1,2,0:T(8,128)(2,1)}), bf16[1,1024,6,1024]{3,1,2,0:T(8,128)(2,1)}) %all-gather.7.cloned.1.call-update) | async-done | bytes 12582928 | tf_op jit(solution)/shard_map/all_gather | solution.py:34
  239.2 32.4 %fusion.10 = f32[256,4,1024]{2,0,1:T(8,128)S(1)} fusion(f32[256,4,1024]{2,0,1:T(8,128)} %fusion.26, bf16[1,1024,6,1024]{3,1,2,0:T(8,128)(2,1)} %all-gather.7.cloned.1.call-done, bf16[256,4,6,1024]{3,2,1,0:T(8,128)(2,1)} %fusion.2), kind=kOutput, calls=%fused_computation.14 | convolution fusion | flops 12886999040 | bytes 33554432 | tf_op jit(solution)/shard_map/asvc,cvy->asy/dot_general | solution.py:31
  271.7 14.8 %convolution_bitcast_fusion.1 = f32[1024,1024]{0,1:T(8,128)S(1)} fusion(f32[256,4,1024]{2,0,1:T(8,128)S(1)} %fusion.10), kind=kOutput, calls=%fused_computation.20 | convolution fusion | flops 12884901888 | bytes 8388608 | tf_op jit(solution)/shard_map/dot_general | solution.py:47
  288.1 90.7 %collective-permute-done.2 = f32[1024,1024]{0,1:T(8,128)S(1)} collective-permute-done((f32[1024,1024]{0,1:T(8,128)S(1)}, f32[1024,1024]{0,1:T(8,128)S(1)}, u32[]{:S(2)}, u32[]{:S(2)}) %collective-permute-start.2) | collective-permute-done | bytes 4194336 | tf_op jit(solution)/shard_map/ppermute | solution.py:52
  383.1 6.8 copy.38
  400.6 72.7 %collective-permute-done.3 = f32[1024,1024]{0,1:T(8,128)} collective-permute-done((f32[1024,1024]{0,1:T(8,128)}, f32[1024,1024]{0,1:T(8,128)}, u32[]{:S(2)}, u32[]{:S(2)}) %collective-permute-start.3) | collective-permute-done | bytes 4194336 | tf_op jit(solution)/shard_map/ppermute | solution.py:52
  473.3 6.8 add.87
  492.0 11.7 %cholesky.223 = f32[128,128]{1,0:T(8,128)S(1)} custom-call(f32[128,128]{1,0:T(8,128)S(1)} %cholesky.580), custom_call_target="Cholesky" | custom-call | tf_op jit(solution)/shard_map/jit(cholesky)/cholesky | solution.py:55
  503.7 9.8 %custom-call.63 = f32[1,128,128]{1,2,0:T(8,128)S(1)} custom-call(f32[1,128,128]{2,1,0:T(8,128)S(1)} %get-tuple-element.74), custom_call_target="InvertDiagBlocksLowerTriangular" | custom-call | tf_op jit(solution)/shard_map/jit(cholesky)/cholesky | solution.py:55
  520.0 11.9 %cholesky.244 = f32[128,128]{1,0:T(8,128)S(1)} custom-call(f32[128,128]{1,0:T(8,128)S(1)} %cholesky.584), custom_call_target="Cholesky" | custom-call | tf_op jit(solution)/shard_map/jit(cholesky)/cholesky | solution.py:55
  532.6 9.8 %custom-call.64 = f32[1,128,128]{1,2,0:T(8,128)S(1)} custom-call(f32[1,128,128]{2,1,0:T(8,128)S(1)} %get-tuple-element.71), custom_call_target="InvertDiagBlocksLowerTriangular" | custom-call | tf_op jit(solution)/shard_map/jit(cholesky)/cholesky | solution.py:55
  545.7 11.7 %cholesky.468 = f32[128,128]{1,0:T(8,128)S(1)} custom-call(f32[128,128]{1,0:T(8,128)S(1)} %cholesky.589), custom_call_target="Cholesky" | custom-call | tf_op jit(solution)/shard_map/jit(cholesky)/cholesky | solution.py:55
  558.7 9.8 %custom-call.65 = f32[1,128,128]{1,2,0:T(8,128)S(1)} custom-call(f32[1,128,128]{2,1,0:T(8,128)S(1)} %get-tuple-element.68), custom_call_target="InvertDiagBlocksLowerTriangular" | custom-call | tf_op jit(solution)/shard_map/jit(cholesky)/cholesky | solution.py:55
  572.0 12.1 %cholesky.487 = f32[128,128]{1,0:T(8,128)S(1)} custom-call(f32[128,128]{1,0:T(8,128)S(1)} %cholesky.594), custom_call_target="Cholesky" | custom-call | tf_op jit(solution)/shard_map/jit(cholesky)/cholesky | solution.py:55
  585.4 9.8 %custom-call.66 = f32[1,128,128]{1,2,0:T(8,128)S(1)} custom-call(f32[1,128,128]{2,1,0:T(8,128)S(1)} %get-tuple-element.65), custom_call_target="InvertDiagBlocksLowerTriangular" | custom-call | tf_op jit(solution)/shard_map/jit(cholesky)/cholesky | solution.py:55
  598.7 11.7 %cholesky.506 = f32[128,128]{1,0:T(8,128)S(1)} custom-call(f32[128,128]{1,0:T(8,128)S(1)} %cholesky.599), custom_call_target="Cholesky" | custom-call | tf_op jit(solution)/shard_map/jit(cholesky)/cholesky | solution.py:55
  611.7 9.9 %custom-call.67 = f32[1,128,128]{1,2,0:T(8,128)S(1)} custom-call(f32[1,128,128]{2,1,0:T(8,128)S(1)} %get-tuple-element.62), custom_call_target="InvertDiagBlocksLowerTriangular" | custom-call | tf_op jit(solution)/shard_map/jit(cholesky)/cholesky | solution.py:55
  625.0 11.7 %cholesky.526 = f32[128,128]{1,0:T(8,128)S(1)} custom-call(f32[128,128]{1,0:T(8,128)S(1)} %cholesky.604), custom_call_target="Cholesky" | custom-call | tf_op jit(solution)/shard_map/jit(cholesky)/cholesky | solution.py:55
  638.0 9.8 %custom-call.68 = f32[1,128,128]{1,2,0:T(8,128)S(1)} custom-call(f32[1,128,128]{2,1,0:T(8,128)S(1)} %get-tuple-element.59), custom_call_target="InvertDiagBlocksLowerTriangular" | custom-call | tf_op jit(solution)/shard_map/jit(cholesky)/cholesky | solution.py:55
  650.8 11.9 %cholesky.546 = f32[128,128]{1,0:T(8,128)S(1)} custom-call(f32[128,128]{1,0:T(8,128)S(1)} %cholesky.609), custom_call_target="Cholesky" | custom-call | tf_op jit(solution)/shard_map/jit(cholesky)/cholesky | solution.py:55
  663.9 9.8 %custom-call.69 = f32[1,128,128]{1,2,0:T(8,128)S(1)} custom-call(f32[1,128,128]{2,1,0:T(8,128)S(1)} %get-tuple-element.56), custom_call_target="InvertDiagBlocksLowerTriangular" | custom-call | tf_op jit(solution)/shard_map/jit(cholesky)/cholesky | solution.py:55
  676.3 11.7 %cholesky.564 = f32[128,128]{1,0:T(8,128)S(1)} custom-call(f32[128,128]{1,0:T(8,128)S(1)} %slice_subtract_fusion.6), custom_call_target="Cholesky" | custom-call | tf_op jit(solution)/shard_map/jit(cholesky)/cholesky | solution.py:55
  695.0 6.7 fusion.11
  701.6 23.0 %while.1 = (s32[]{:T(128)}, f32[1024,1024]{1,0:T(8,128)}, s32[8,2]{0,1:T(2,128)S(1)}, f32[8,128,128]{2,1,0:T(8,128)S(1)}, s32[]{:T(128)}) while((s32[]{:T(128)}, f32[1024,1024]{1,0:T(8,128)}, s32[8,2]{0,1:T(2,128)S(1)}, f32[8,128,128]{2,1,0:T(8,128)S(1)}, s32[]{:T(128)}) %tuple.65), condition=%wide.while_cond, body=%wide.while_body.sunk | while | flops 2 | bytes 131181 | solution.py:56
  724.7 79.0 %custom-call.70 = f32[8,128,128]{1,2,0:T(8,128)S(1)} custom-call(f32[8,128,128]{2,1,0:T(8,128)S(1)} %get-tuple-element.9), custom_call_target="InvertDiagBlocksLowerTriangular" | custom-call | tf_op jit(solution)/shard_map/jit(_solve_triangular)/triangular_solve | solution.py:56
  (114 shorter events, 135.0 us)
Async XLA Ops:
  7.2 30.0 %copy-start = (bf16[1,1024,4,256]{3,2,1,0:T(4,128)(2,1)S(1)}, bf16[1,1024,4,256]{3,2,1,0:T(4,128)(2,1)}, u32[]{:S(2)}) copy-start(bf16[1,1024,4,256]{3,2,1,0:T(4,128)(2,1)} %param.10) | copy-start | bytes 6291460
  7.2 107.8 %all-gather.5.cloned.1.call-start = ((), (), s32[]{:S(2)}) async-start(), calls=%async_computation.1 | async-start | bytes 10485760 | tf_op jit(solution)/shard_map/all_gather | solution.py:22
  7.9 231.3 %all-gather.7.cloned.1.call-start = ((), (), s32[]{:S(2)}) async-start(), calls=%async_computation.2 | async-start | bytes 15728640 | tf_op jit(solution)/shard_map/all_gather | solution.py:34
  8.7 28.5 %collective-permute-start.1 = (bf16[1024,1024]{1,0:T(8,128)(2,1)}, bf16[1024,1024]{1,0:T(8,128)(2,1)S(1)}, u32[]{:S(2)}, u32[]{:S(2)}) collective-permute-start(bf16[1024,1024]{1,0:T(8,128)(2,1)} %bitcast.188), channel_id=1, source_target_pairs={{28,0},{0,4},{4,8},{8,12},{12,16},{16,20},{20,24},{24,28},{29,1},{... | collective-permute-start | bytes 6291464 | tf_op jit(solution)/shard_map/ppermute | solution.py:14
  9.2 119.9 %collective-permute-start = (bf16[256,6,1024]{2,0,1:T(8,128)(2,1)}, bf16[256,6,1024]{2,0,1:T(8,128)(2,1)}, u32[]{:S(2)}, u32[]{:S(2)}) collective-permute-start(bf16[256,6,1024]{2,0,1:T(8,128)(2,1)} %bitcast.187), channel_id=1, source_target_pairs={{28,0},{0,4},{4,8},{8,12},{12,16},{16,20},{20,24},{24,28},{29,1},{... | collective-permute-start | bytes 9437192 | tf_op jit(solution)/shard_map/ppermute | solution.py:14
  129.1 21.9 %copy-start.5 = (bf16[1,6,6,4,4]{2,4,3,1,0:T(4,128)(2,1)S(1)}, bf16[1,6,6,4,4]{2,4,3,1,0:T(4,128)(2,1)}, u32[]{:S(2)}) copy-start(bf16[1,6,6,4,4]{2,4,3,1,0:T(4,128)(2,1)} %param.11) | copy-start | bytes 3460
  271.7 14.8 %copy-start.4 = (f32[256,4,1024]{2,0,1:T(8,128)}, f32[256,4,1024]{2,0,1:T(8,128)S(1)}, u32[]{:S(2)}) copy-start(f32[256,4,1024]{2,0,1:T(8,128)S(1)} %fusion.10) | copy-start | bytes 12582916
  286.5 92.2 %collective-permute-start.2 = (f32[1024,1024]{0,1:T(8,128)S(1)}, f32[1024,1024]{0,1:T(8,128)S(1)}, u32[]{:S(2)}, u32[]{:S(2)}) collective-permute-start(f32[1024,1024]{0,1:T(8,128)S(1)} %convolution_bitcast_fusion.1), channel_id=1, source_target_pairs={{0,1},{1,0},{2,3},{3,2},{4,5},{5,4},{6,7},{7,6},{8,9},{9,8},{10,11... | collective-permute-start | bytes 12582920 | tf_op jit(solution)/shard_map/ppermute | solution.py:52
  381.7 91.6 %collective-permute-start.3 = (f32[1024,1024]{0,1:T(8,128)}, f32[1024,1024]{0,1:T(8,128)}, u32[]{:S(2)}, u32[]{:S(2)}) collective-permute-start(f32[1024,1024]{0,1:T(8,128)} %add.86), channel_id=1, source_target_pairs={{0,2},{1,3},{2,0},{3,1},{4,6},{5,7},{6,4},{7,5},{8,10},{9,11},{10,... | collective-permute-start | bytes 12582920 | tf_op jit(solution)/shard_map/ppermute | solution.py:52
  490.0 2.0 copy-start.3
  803.7 4.3 copy-start.2
  828.9 10.8 %copy-start.1 = (bf16[1,1024,4,256]{3,2,1,0:T(4,128)(2,1)S(1)}, bf16[1,1024,4,256]{3,2,1,0:T(4,128)(2,1)}, u32[]{:S(2)}) copy-start(bf16[1,1024,4,256]{3,2,1,0:T(4,128)(2,1)} %param.10) | copy-start | bytes 6291460
Sparse Core Ops, SparseCore 0:
  9.8 105.0 all-gather.4
  116.8 122.3 all-gather.6
